TPU v7x, 32 devices: a whole 2x2x4 slice. The times are simulated.
32 devices in a mesh: modes: 4 (over y, core), gz: 8 (over z, x).
Axes of the slice: x: 2, y: 2, z: 4, core: 2. Of those that a mesh axis runs over, the one named last changes fastest.
Arguments:
- source_field: float32 [128, 2, 8, 2048], P('gz', None, None, 'modes'), may hold values from -0.075 to 0.075
- coupling_below: float32 [128], P('gz'), may hold values from 0.5 to 2
- coupling_above: float32 [128], P('gz'), may hold values from 0.5 to 2
- eigen_stream: float32 [8], replicated, may hold values from 0.000390625 to 0.015625
- eigen_span: float32 [2048], replicated, may hold values from 0.000390625 to 0.015625
Outputs:
- pressure: float32 [128, 2, 8, 2048], P('gz', None, 'modes')
All inputs are finite; a program needn't handle non-finite values.
Results may differ from a plain program's by a relative error of at most 0.0003.
Values sent between devices are 32-bit elements; how exact they have to be, the bound alone decides.
No kernel may reach another device: no remote copies, remote signals or barrier semaphores. Data moves between devices by JAX's collectives and lax.ppermute only.
A program may use at most 64 MiB of HBM per device.

v0:
```python
import jax
import jax.numpy as jnp
from jax import lax
from jax.sharding import PartitionSpec as P


def shifted(array, axis, by):
    count = lax.axis_size(axis)
    pairs = [(i, i + by) for i in range(count) if 0 <= i + by < count]
    return lax.ppermute(array, axis, pairs)


def thomas(lower_row, upper_row, spectral, sources, initial):
    row_count = sources.shape[0]

    def thomas_forward(carried, inputs):
        factor, partial_value = carried
        lower_val, upper_val, source_row = inputs
        pivots = lower_val + upper_val + spectral - lower_val * factor
        partial_value = (source_row + lower_val * partial_value) / pivots
        factor = upper_val / pivots
        return ((factor, partial_value), (factor, partial_value))

    _, (factors, partials) = lax.scan(
        thomas_forward,
        (jnp.zeros_like(spectral), initial),
        (lower_row, upper_row, sources),
        unroll=True,
    )
    retain = (jnp.arange(row_count) < row_count - 1).astype(jnp.float32)
    factors = factors * retain.reshape((row_count,) + (1,) * spectral.ndim)

    def thomas_backward(behind, inputs):
        factor, partial_value = inputs
        result = partial_value + factor * behind
        return (result, result)

    _, solved = lax.scan(
        thomas_backward, jnp.zeros_like(initial), (factors, partials), reverse=True, unroll=True
    )
    return solved


def reduced_solve(coeffs, right_side):

    def reduced_forward(carried, inputs):
        factor, partial_value = carried
        coeff_row, right_row = inputs
        pivots = coeff_row[1] - coeff_row[0] * factor
        factor = coeff_row[2] / pivots
        partial_value = (right_row - coeff_row[0] * partial_value) / pivots
        return ((factor, partial_value), (factor, partial_value))

    initial = (jnp.zeros_like(coeffs[0, 0]), jnp.zeros_like(right_side[0]))
    _, (factors, partials) = lax.scan(reduced_forward, initial, (coeffs, right_side), unroll=True)

    def reduced_backward(behind, inputs):
        factor, partial_value = inputs
        result = partial_value - factor * behind
        return (result, result)

    _, values = lax.scan(
        reduced_backward,
        jnp.zeros_like(right_side[0]),
        (factors, partials),
        reverse=True,
        unroll=True,
    )
    return values


def interfaces(planes, lower_row, upper_row, spectral):
    row_count = planes.shape[0]
    interior = row_count - 1
    modes_flat = planes.shape[2]
    last_mask = (jnp.arange(interior) == interior - 1).astype(jnp.float32) * upper_row[:interior]
    extra_source = last_mask[:, None, None] * jnp.ones((1, 1, modes_flat), jnp.float32)
    sources = jnp.concatenate(
        [planes[:interior], jnp.zeros((interior, 1, modes_flat), jnp.float32), extra_source], axis=1
    )
    initial = jnp.zeros((4, modes_flat), jnp.float32).at[2].set(1.0)
    solved = thomas(lower_row[:interior], upper_row[:interior], spectral, sources, initial)
    from_above = shifted(solved[0], "gz", -1)
    last_row = solved[interior - 1]
    lower_last = lower_row[row_count - 1]
    upper_last = upper_row[row_count - 1]
    coupling_down = -lower_last * last_row[2]
    central = (
        lower_last + upper_last + spectral - lower_last * last_row[3] - upper_last * from_above[2]
    )
    coupling_up = -upper_last * from_above[3]
    right_side = planes[row_count - 1] + lower_last * last_row[:2] + upper_last * from_above[:2]
    coeffs = jnp.stack([coupling_down, central, coupling_up])
    return (solved, coeffs, right_side)


def assemble(solved, interface_values):
    own_value = interface_values[:2]
    prev_value = interface_values[2:]
    inner = solved[:, :2] + solved[:, 2:3] * prev_value[None] + solved[:, 3:4] * own_value[None]
    return jnp.concatenate([inner, own_value[None]], axis=0)


def per_device(source_field, coupling_below, coupling_above, eigen_stream, eigen_span):
    arrived = lax.all_to_all(source_field, "modes", split_axis=2, concat_axis=3, tiled=True)
    row_count, _, kx_count, ky_count = arrived.shape
    partitions = lax.axis_size("gz")
    gz_index = lax.axis_index("gz")
    offset = lax.axis_index("modes") * kx_count
    stream_part = lax.dynamic_slice_in_dim(eigen_stream, offset, kx_count)
    spectral = stream_part[:, None] + eigen_span[None, :]
    global_row = gz_index * row_count + jnp.arange(row_count)
    lower_row = jnp.where(global_row == 0, 0.0, coupling_below)
    upper_row = jnp.where(global_row == row_count * partitions - 1, 0.0, coupling_above)
    modes_flat = kx_count * ky_count
    planes = arrived.reshape(row_count, 2, modes_flat)
    solved, coeffs, right_side = interfaces(planes, lower_row, upper_row, spectral.reshape(-1))
    coeff_items = coeffs.reshape(1, 3, kx_count, ky_count)
    right_items = right_side.reshape(1, 2, kx_count, ky_count)
    values = reduced_solve(
        lax.all_to_all(coeff_items, "gz", split_axis=3, concat_axis=0, tiled=True),
        lax.all_to_all(right_items, "gz", split_axis=3, concat_axis=0, tiled=True),
    )
    below_values = jnp.concatenate([jnp.zeros_like(values[:1]), values[:-1]], axis=0)
    paired = jnp.concatenate([values, below_values], axis=1)
    interface_values = lax.all_to_all(paired, "gz", split_axis=0, concat_axis=3, tiled=True)
    pressure = assemble(solved, interface_values.reshape(4, modes_flat))
    return pressure.reshape(row_count, 2, kx_count, ky_count)


def solution(mesh):
    in_specs = (P("gz", None, None, "modes"), P("gz"), P("gz"), P(), P())
    out_specs = P("gz", None, "modes", None)
    return jax.shard_map(
        per_device, mesh=mesh, in_specs=in_specs, out_specs=out_specs, check_vma=False
    )
```

profile of v0, /device:TPU:0, one launch (start us, length us, event | category | flops | bytes accessed | tf_op | source)
XLA Modules:
  0.0 153.8 jit_solution(18007086466472637981)
XLA Ops:
  0.0 2.2 %copy.91 = f32[16,2,8,512]{3,0,1,2:T(8,128)} copy(f32[16,2,8,512]{3,2,1,0:T(8,128)} %param.7) | data formatting | bytes 1048576 | tf_op args[0]
  2.2 4.3 %all-to-all-start = ((f32[16,2,8,512]{3,0,1,2:T(8,128)}), f32[16,2,8,512]{3,0,1,2:T(8,128)S(1)}, u32[]{:S(2)}, u32[]{:S(2)}) async-start(f32[16,2,8,512]{3,0,1,2:T(8,128)} %copy.91), calls=%async_computation | async-start | bytes 1048576 | tf_op jit(solution)/shard_map/all_to_all | solution.py:105
  6.5 0.7 fusion.116
  7.9 0.7 fusion.117
  12.3 0.8 divide_bitcast_fusion
  31.2 17.7 %subtract_divide_fusion = (f32[1,4096]{1,0:T(1,128)S(1)}, f32[1,4096]{1,0:T(1,128)S(1)}, f32[1,4096]{1,0:T(1,128)S(1)}, f32[1,4096]{1,0:T(1,128)S(1)}, f32[1,409...) fusion(f32[1,4096]{1,0:T(1,128)S(1)} %bitcast.585, ...), kind=kLoop, calls=%fused_computation.174 | loop fusion | flops 172032 | bytes 475248 | tf_op jit(solution)/shard_map/eval_jaxpr/div | solution.py:21
  49.8 17.6 %multiply_subtract_fusion = (f32[4096]{0:T(1024)S(1)}, f32[4096]{0:T(1024)S(1)}, f32[4096]{0:T(1024)S(1)}, f32[4096]{0:T(1024)S(1)}, f32[4096]{0:T(1024)S(1)}, /...) fusion(f32[4096]{0:T(1024)S(1)} %bitcast.584, ...), kind=kLoop, calls=%fused_computation.160 | loop fusion | flops 172032 | bytes 475248 | tf_op jit(solution)/shard_map/eval_jaxpr/sub | solution.py:19
  67.9 0.5 slice.459
  69.1 9.6 %multiply_add_fusion = (f32[4,4096]{1,0:T(4,128)S(1)}, f32[4,4096]{1,0:T(4,128)S(1)}) fusion(f32[4096]{0:T(1024)S(1)} %bitcast.545, f32[4096]{0:T(1024)S(1)} %bitcast.554, f32[4096]{0:T(1024)S(1)} %bitcast.527, f32[4096]{0:T(1024)S(1)} %bitcast.556, f32[4096]{0:T(1024)S(1)} %bitcast.530, f32[4096]{0:T(1024)S(1)} %bitcast.558, f32[4096]{0:T(1024)S(1)} %bitcast.533, ...), kind=kLoop, calls=%fused_computation.56 | loop fusion | flops 1212416 | bytes 1671228 | tf_op jit(solution)/shard_map/eval_jaxpr/add | solution.py:35
  78.7 1.3 collective-permute-start
  80.0 10.3 %add_dynamic-update-slice_fusion = (f32[15,4,4096]{2,1,0:T(4,128)}, f32[1,4,4096]{2,1,0:T(4,128)S(1)}, f32[1,4,4096]{2,1,0:T(4,128)S(1)}, f32[1,4,4096]{2,1,0:T(...) fusion(f32[4096]{0:T(1024)S(1)} %bitcast.567, ...), kind=kLoop, calls=%fused_computation.57 | loop fusion | flops 1212415 | bytes 2457660
  90.3 0.6 constant_dynamic-update-slice_fusion.13
  90.9 0.6 constant_dynamic-update-slice_fusion.12
  91.5 0.6 constant_dynamic-update-slice_fusion.11
  92.2 0.6 constant_dynamic-update-slice_fusion.10
  92.8 0.6 constant_dynamic-update-slice_fusion.9
  93.4 0.6 constant_dynamic-update-slice_fusion.8
  94.1 0.6 constant_dynamic-update-slice_fusion.7
  94.7 0.6 constant_dynamic-update-slice_fusion.6
  95.3 0.7 constant_dynamic-update-slice_fusion.5
  96.0 0.6 constant_dynamic-update-slice_fusion.4
  96.6 0.6 constant_dynamic-update-slice_fusion.3
  97.3 0.6 constant_dynamic-update-slice_fusion.2
  97.9 1.2 constant_dynamic-update-slice_fusion.1
  99.1 1.4 fusion.53
  100.6 1.3 fusion.18
  102.0 1.1 copy.93
  103.1 3.5 %reshape.3546 = f32[8,1,1024]{2,1,0:T(1,128)} reshape(f32[2048,1,2,2]{3,2,1,0:T(2,128)S(1)} %bitcast.511) | data formatting | bytes 65536
  106.6 7.7 %all-to-all-start.1 = ((f32[8,1,1024]{2,1,0:T(1,128)}), f32[8,1,1024]{2,1,0:T(1,128)S(1)}, u32[]{:S(2)}, u32[]{:S(2)}) async-start(f32[8,1,1024]{2,1,0:T(1,128)} %reshape.3546), calls=%async_computation.1 | async-start | bytes 65536 | tf_op jit(solution)/shard_map/all_to_all | solution.py:122
  114.3 1.1 copy.95
  115.4 3.6 %reshape.3548 = f32[8,1,1536]{2,1,0:T(1,128)} reshape(f32[2048,1,2,3]{3,2,1,0:T(2,128)S(1)} %bitcast.512) | data formatting | bytes 98304
  119.0 1.9 %all-to-all-done.1 = f32[8,1,1024]{2,1,0:T(1,128)S(1)} async-done(((f32[8,1,1024]{2,1,0:T(1,128)}), f32[8,1,1024]{2,1,0:T(1,128)S(1)}, u32[]{:S(2)}, u32[]{:S(2)}) %all-to-all-start.1) | async-done | bytes 32800 | tf_op jit(solution)/shard_map/all_to_all | solution.py:122
  121.0 4.1 %all-to-all-start.2 = ((f32[8,1,1536]{2,1,0:T(1,128)}), f32[8,1,1536]{2,1,0:T(1,128)S(1)}, u32[]{:S(2)}, u32[]{:S(2)}) async-start(f32[8,1,1536]{2,1,0:T(1,128)} %reshape.3548), calls=%async_computation.2 | async-start | bytes 98304 | tf_op jit(solution)/shard_map/all_to_all | solution.py:121
  125.0 1.2 constant_dynamic-update-slice_fusion
  126.2 0.5 broadcast.5415
  126.7 0.7 reduce.15
  127.5 3.2 %reshape.3547 = f32[2048,1,2,2]{3,2,1,0:T(2,128)S(1)} reshape(f32[8,1024]{1,0:T(8,128)S(1)} %reduce.15) | data formatting | bytes 65536
  130.7 0.9 copy.94
  131.8 0.7 reduce.14
  132.6 3.1 %reshape.3549 = f32[2048,1,2,3]{3,2,1,0:T(2,128)S(1)} reshape(f32[8,1536]{1,0:T(8,128)S(1)} %reduce.14) | data formatting | bytes 98304
  135.7 0.8 copy.123
  137.0 0.6 fusion.1
  137.6 5.8 %all-to-all-start.3 = ((f32[8,4,2,256]{3,2,1,0:T(2,128)}), f32[8,4,2,256]{3,2,1,0:T(2,128)S(1)}, u32[]{:S(2)}, u32[]{:S(2)}) async-start(f32[8,4,2,256]{3,2,1,0:T(2,128)} %fusion.1), calls=%async_computation.3 | async-start | bytes 131072 | tf_op jit(solution)/shard_map/all_to_all | solution.py:126
  143.4 2.0 %fusion.112 = (f32[15,1,4096]{2,1,0:T(1,128)S(1)}, f32[15,1,4096]{2,1,0:T(1,128)S(1)}) fusion(f32[15,4,4096]{2,1,0:T(4,128)} %constant_dynamic-update-slice_fusion), kind=kLoop, calls=%fused_computation.270 | loop fusion | bytes 983040 | tf_op jit(solution)/shard_map/slice | solution.py:100
  145.8 4.5 %all-to-all-done.3 = f32[8,4,2,256]{3,2,1,0:T(2,128)S(1)} async-done(((f32[8,4,2,256]{3,2,1,0:T(2,128)}), f32[8,4,2,256]{3,2,1,0:T(2,128)S(1)}, u32[]{:S(2)}, u32[]{:S(2)}) %all-to-all-start.3) | async-done | bytes 65568 | tf_op jit(solution)/shard_map/all_to_all | solution.py:126
  150.5 1.6 %fusion = f32[15,2,4096]{2,1,0:T(2,128)S(1)} fusion(f32[15,4,4096]{2,1,0:T(4,128)} %constant_dynamic-update-slice_fusion, f32[2,4096]{1,0:T(2,128)S(1)} %mul.2749, f32[15,4096]{1,0:T(8,128)S(1)} %bitcast.519, f32[2,4096]{1,0:T(2,128)S(1)} %mul.2744, f32[15,4096]{1,0:T(8,128)S(1)} %bitcast.518), kind=kLoop, calls=%fused_computation.4 | loop fusion | flops 491520 | bytes 1540096 | tf_op jit(solution)/shard_map/add | solution.py:100
  152.0 0.6 concatenate.39
  152.6 1.1 pad_maximum_fusion.1
  (95 shorter events, 3.6 us)
Async XLA Ops:
  0.0 6.5 %copy-start.4 = (f32[16]{0:T(128)S(1)}, f32[16]{0:T(128)}, u32[]{:S(2)}) copy-start(f32[16]{0:T(128)} %param.9) | copy-start | bytes 196
  0.0 6.5 %copy-start.3 = (f32[16]{0:T(128)S(1)}, f32[16]{0:T(128)}, u32[]{:S(2)}) copy-start(f32[16]{0:T(128)} %param.8) | copy-start | bytes 196
  0.0 12.2 %copy-start.5 = (f32[8]{0:T(128)S(1)}, f32[8]{0:T(128)}, u32[]{:S(2)}) copy-start(f32[8]{0:T(128)} %param.10) | copy-start | bytes 100
  0.0 12.3 %copy-start.2 = (f32[2048]{0:T(1024)S(1)}, f32[2048]{0:T(1024)}, u32[]{:S(2)}) copy-start(f32[2048]{0:T(1024)} %param.11) | copy-start | bytes 24580
  2.2 65.2 %all-to-all-start = ((f32[16,2,8,512]{3,0,1,2:T(8,128)}), f32[16,2,8,512]{3,0,1,2:T(8,128)S(1)}, u32[]{:S(2)}, u32[]{:S(2)}) async-start(f32[16,2,8,512]{3,0,1,2:T(8,128)} %copy.91), calls=%async_computation | async-start | bytes 1048576 | tf_op jit(solution)/shard_map/all_to_all | solution.py:105
  67.8 1.3 copy-start.1
  68.4 11.6 %copy-start = (f32[1,4,4096]{2,1,0:T(4,128)S(1)}, f32[1,4,4096]{2,1,0:T(4,128)}, u32[]{:S(2)}) copy-start(f32[1,4,4096]{2,1,0:T(4,128)} %constant.75.clone.1) | copy-start | bytes 196612
  78.7 20.5 %collective-permute-start = (f32[4,4096]{1,0:T(4,128)S(1)}, f32[4,4096]{1,0:T(4,128)S(1)}, u32[]{:S(2)}, u32[]{:S(2)}) collective-permute-start(f32[4,4096]{1,0:T(4,128)S(1)} %get-tuple-element.64), channel_id=1, source_target_pairs={{1,0},{2,1},{3,2},{4,3},{5,4},{6,5},{7,6},{9,8},{10,9},{11,10},{12... | collective-permute-start | bytes 196616 | tf_op jit(solution)/shard_map/ppermute | solution.py:10
  106.6 14.4 %all-to-all-start.1 = ((f32[8,1,1024]{2,1,0:T(1,128)}), f32[8,1,1024]{2,1,0:T(1,128)S(1)}, u32[]{:S(2)}, u32[]{:S(2)}) async-start(f32[8,1,1024]{2,1,0:T(1,128)} %reshape.3546), calls=%async_computation.1 | async-start | bytes 65536 | tf_op jit(solution)/shard_map/all_to_all | solution.py:122
  121.0 10.9 %all-to-all-start.2 = ((f32[8,1,1536]{2,1,0:T(1,128)}), f32[8,1,1536]{2,1,0:T(1,128)S(1)}, u32[]{:S(2)}, u32[]{:S(2)}) async-start(f32[8,1,1536]{2,1,0:T(1,128)} %reshape.3548), calls=%async_computation.2 | async-start | bytes 98304 | tf_op jit(solution)/shard_map/all_to_all | solution.py:121
  137.6 12.7 %all-to-all-start.3 = ((f32[8,4,2,256]{3,2,1,0:T(2,128)}), f32[8,4,2,256]{3,2,1,0:T(2,128)S(1)}, u32[]{:S(2)}, u32[]{:S(2)}) async-start(f32[8,4,2,256]{3,2,1,0:T(2,128)} %fusion.1), calls=%async_computation.3 | async-start | bytes 131072 | tf_op jit(solution)/shard_map/all_to_all | solution.py:126
where the time goes:
time: 155 us; the launch traced here: 154 us
  other arithmetic  71 us (46%)
  local copies, waits for them, and re-layouts  30.6 us (20%)
  starting transfers between devices  23.1 us (15%)
  between operations  22.5 us (15%)
  waiting for transfers between devices  6.71 us (4%)
    unnamed x69, local copies, waits for them, and re-layouts  20.1 us
    div x1, other arithmetic, thomas_forward(): factor = upper_val / pivots  17.7 us
    sub x1, other arithmetic, thomas_forward(): pivots = lower_val + upper_val + spectral - lower_val * factor  17.6 us
    unnamed x12, other arithmetic  16.4 us
    add x1, other arithmetic, thomas_backward(): result = partial_value + factor * behind  9.6 us
    all_to_all x1, starting transfers between devices, per_device(): lax.all_to_all(right_items, 'gz', split_axis=3, concat_axis=0, tiled=True)  7.67 us
    all_to_all x1, starting transfers between devices, per_device(): lax.all_to_all(paired, 'gz', split_axis=0, concat_axis=3, tiled=True)  5.8 us
    all_to_all x1, waiting for transfers between devices, per_device(): lax.all_to_all(paired, 'gz', split_axis=0, concat_axis=3, tiled=True)  4.54 us
  transfers between devices with their start and end apart: 5, of which 3 were waited for; matrix products, arithmetic and copies ran while one was open for 47% of the time, Pallas kernels for 0%

commit v1 on v0

v1 whole, which is shorter than its diff:
```python
import functools

import jax
import jax.numpy as jnp
from jax import lax
from jax.experimental import pallas as pl
from jax.experimental.pallas import tpu as pltpu
from jax.sharding import PartitionSpec as P

LANES = 128


def total(axis_size):
    return axis_size


def reduce_kernel(sizes, lower_ref, upper_ref, stream_ref, span_ref, source_ref, ports_ref, couple_ref):
    mode_count, rows, kx_count, tiles = sizes
    me = lax.axis_index("modes")
    lower = [lower_ref[k] for k in range(rows)]
    upper = [upper_ref[k] for k in range(rows)]
    lane = lax.broadcasted_iota(jnp.int32, (8, LANES), 1)
    sub = lax.broadcasted_iota(jnp.int32, (8, LANES), 0)
    table = jnp.zeros((8, LANES), jnp.float32)
    for k in range(rows):
        table = jnp.where((lane == k) & (sub == 0), lower[k], table)
        table = jnp.where((lane == k) & (sub == 1), upper[k], table)
    couple_ref[...] = table
    for dest in range(mode_count):
        spectral = spectral_block(sizes, stream_ref, span_ref, dest, me)
        grown = jnp.ones_like(spectral)
        passed = jnp.ones_like(spectral)
        partial = [jnp.zeros_like(spectral)] * 2
        first = [jnp.zeros_like(spectral)] * 2
        for k in range(rows):
            held = spectral + lower[k] * grown
            inverse = 1.0 / (upper[k] + held)
            factor = upper[k] * inverse
            grown = held * inverse
            for c in range(2):
                partial[c] = (source_ref[dest, k, c] + lower[k] * partial[c]) * inverse
                first[c] = first[c] + passed * partial[c]
            passed = passed * factor
        for c in range(2):
            ports_ref[dest, c] = first[c]
            ports_ref[dest, 2 + c] = partial[c]


def spectral_block(sizes, stream_ref, span_ref, dest, origin):
    _, _, kx_count, tiles = sizes
    height = tiles * kx_count
    sub = lax.broadcasted_iota(jnp.int32, (height, LANES), 0)
    streamwise = jnp.zeros((height, LANES), jnp.float32)
    for j in range(kx_count):
        streamwise = jnp.where(sub % kx_count == j, stream_ref[dest * kx_count + j], streamwise)
    spanwise = jnp.zeros((height, LANES), jnp.float32)
    for t in range(tiles):
        row = span_ref[pl.ds(origin * tiles + t, 1), :]
        spanwise = jnp.where(sub // kx_count == t, jnp.broadcast_to(row, (height, LANES)), spanwise)
    return streamwise + spanwise


def spread(table, i, k, shape):
    return jnp.broadcast_to(table[i : i + 1, k : k + 1], shape)


def climb(spectral, state, below, above):
    num, den = state
    product = None
    for near, far in zip(below, above):
        num = spectral * den + near * num
        before = den
        den = num + far * den
        product = near if product is None else product * near
    return num, den, far * before, product


def merge_kernel(sizes, stream_ref, span_ref, own_ref, pair_ref, own_table, pair_table, merged_ref, table_ref):
    mode_count, rows, kx_count, tiles = sizes
    shape = (tiles * kx_count, LANES)
    me = lax.axis_index("modes")
    upside = lax.axis_index("gz") % 2 == 1
    own, pair = own_table[...], pair_table[...]
    low_table = jnp.where(upside, pair, own)
    high_table = jnp.where(upside, own, pair)
    sub = lax.broadcasted_iota(jnp.int32, (8, LANES), 0)
    table_ref[...] = jnp.where(sub < 2, low_table, pltpu.roll(high_table, 2, 0))
    low_l = [spread(low_table, 0, k, shape) for k in range(rows)]
    low_u = [spread(low_table, 1, k, shape) for k in range(rows)]
    high_l = [spread(high_table, 0, k, shape) for k in range(rows)]
    high_u = [spread(high_table, 1, k, shape) for k in range(rows)]
    for d in range(mode_count):
        spectral = spectral_block(sizes, stream_ref, span_ref, me, me ^ d)
        one = jnp.ones(shape, jnp.float32)
        own_ports = [own_ref[d, i] for i in range(4)]
        pair_ports = [pair_ref[d, i] for i in range(4)]
        low = [jnp.where(upside, b, a) for a, b in zip(own_ports, pair_ports)]
        high = [jnp.where(upside, a, b) for a, b in zip(own_ports, pair_ports)]
        num, den, tail, _ = climb(spectral, (one, one), low_l, low_u)
        passed = tail / den
        _, den_all, _, product = climb(spectral, (num, den), high_l, high_u)
        ratio = product * den / den_all
        for c in range(2):
            merged_ref[d, 2 + c] = high[2 + c] + ratio * (low[2 + c] + passed * high[c])
        num, den, tail, _ = climb(spectral, (one, one), high_u[::-1], high_l[::-1])
        passed = tail / den
        _, den_all, _, product = climb(spectral, (num, den), low_u[::-1], low_l[::-1])
        ratio = product * den / den_all
        for c in range(2):
            merged_ref[d, c] = low[c] + ratio * (high[c] + passed * low[2 + c])


def final_kernel(sizes, pairs, lower_ref, upper_ref, stream_ref, span_ref, pair_ref, pair_table, *rest):
    mode_count, rows, kx_count, tiles = sizes
    shape = (tiles * kx_count, LANES)
    others = rest[: pairs - 1]
    tables = rest[pairs - 1 : 2 * (pairs - 1)]
    sources = rest[2 * (pairs - 1) : 2 * (pairs - 1) + mode_count]
    out_ref, factor_ref = rest[2 * (pairs - 1) + mode_count :]
    me = lax.axis_index("modes")
    partition = lax.axis_index("gz")
    upside = partition % 2 == 1
    level = partition // 2
    one = jnp.ones(shape, jnp.float32)
    zero = jnp.zeros(shape, jnp.float32)
    spectral = [spectral_block(sizes, stream_ref, span_ref, me, me ^ d) for d in range(mode_count)]
    start = ((one,) * mode_count, (zero,) * mode_count, (zero,) * (2 * mode_count))

    def enter(state, ports, enters, leaves, near, far):
        grown, passed, partial = state
        new_grown, new_passed, new_partial = [], [], []
        for d in range(mode_count):
            num, den, tail, product = climb(spectral[d], (grown[d], one), near, far)
            inverse = 1.0 / den
            ratio = product * inverse
            new_grown.append(num * inverse)
            new_passed.append(tail * inverse)
            for c in range(2):
                new_partial.append(
                    ports[d, leaves + c] + ratio * (partial[2 * d + c] + passed[d] * ports[d, enters + c])
                )
        return tuple(new_grown), tuple(new_passed), tuple(new_partial)

    def rows_of(table, which):
        low = [spread(table, i, k, shape) for i in which for k in range(rows)]
        return low

    def up(state, ports, table, blocks):
        near = rows_of(table, [2 * b for b in blocks])
        far = rows_of(table, [2 * b + 1 for b in blocks])
        return enter(state, ports, 0, 2, near, far)

    def down(state, ports, table, blocks):
        near = rows_of(table, [2 * b + 1 for b in blocks])[::-1]
        far = rows_of(table, [2 * b for b in blocks])[::-1]
        return enter(state, ports, 2, 0, near, far)

    from_below, from_above = start, start
    for d in range(pairs - 1, 0, -1):
        from_below = lax.cond(
            level >= d,
            lambda s, d=d: up(s, others[d - 1], tables[d - 1][...], (0, 1)),
            lambda s: s,
            from_below,
        )
    for d in range(1, pairs):
        from_above = lax.cond(
            level < d,
            lambda s, d=d: down(s, others[d - 1], tables[d - 1][...], (0, 1)),
            lambda s: s,
            from_above,
        )
    from_below = lax.cond(
        upside, lambda s: up(s, pair_ref, pair_table[...], (0,)), lambda s: s, from_below
    )
    from_above = lax.cond(
        upside, lambda s: s, lambda s: down(s, pair_ref, pair_table[...], (0,)), from_above
    )
    lower = [lower_ref[k] for k in range(rows)]
    upper = [upper_ref[k] for k in range(rows)]
    for d in range(mode_count):
        at = me ^ d
        grown = from_below[0][d]
        partial = list(from_below[2][2 * d : 2 * d + 2])
        for k in range(rows):
            held = spectral[d] + lower[k] * grown
            inverse = 1.0 / (upper[k] + held)
            factor = upper[k] * inverse
            grown = held * inverse
            factor_ref[k, d] = factor
            for c in range(2):
                partial[c] = (sources[d][k, c] + lower[k] * partial[c]) * inverse
                out_ref[k, c, at] = partial[c]
        rest_of = 1.0 / (grown + factor * from_above[0][d])
        for c in range(2):
            value = (partial[c] + factor * from_above[2][2 * d + c]) * rest_of
            out_ref[rows - 1, c, at] = value
            for k in range(rows - 2, -1, -1):
                value = out_ref[k, c, at] + factor_ref[k, d] * value
                out_ref[k, c, at] = value


SMEM = pl.BlockSpec(memory_space=pltpu.SMEM)
VMEM = pl.BlockSpec(memory_space=pltpu.VMEM)


def per_device(source_field, coupling_below, coupling_above, eigen_stream, eigen_span):
    rows, _, kx_total, ky_local = source_field.shape
    mode_count = lax.axis_size("modes")
    partitions = lax.axis_size("gz")
    chips = mode_count // 2
    pairs = partitions // 2
    kx_count = kx_total // mode_count
    tiles = ky_local // LANES
    height = tiles * kx_count
    sizes = (mode_count, rows, kx_count, tiles)
    me = lax.axis_index("modes")
    partition = lax.axis_index("gz")
    global_row = partition * rows + jnp.arange(rows)
    lower = jnp.where(global_row == 0, 0.0, coupling_below)
    upper = jnp.where(global_row == rows * partitions - 1, 0.0, coupling_above)
    span = eigen_span.reshape(-1, LANES)

    def move(array, modes_by=0, pair=0, level=0):
        links = []
        for m in range(mode_count):
            for g in range(partitions):
                to = ((g // 2 + level) % pairs) * 2 + ((g % 2) ^ pair)
                links.append((m * partitions + g, (m ^ modes_by) * partitions + to))
        return lax.ppermute(array, ("modes", "gz"), links)

    def piece(array, index):
        return lax.dynamic_index_in_dim(array, index, 0, keepdims=False)

    blocks = source_field.reshape(rows, 2, mode_count, kx_count, tiles, LANES)
    blocks = blocks.transpose(2, 0, 1, 4, 3, 5).reshape(mode_count, rows, 2, height, LANES)
    block_shape = jax.ShapeDtypeStruct((mode_count, 4, height, LANES), jnp.float32)
    table_shape = jax.ShapeDtypeStruct((8, LANES), jnp.float32)
    ports, table = pl.pallas_call(
        functools.partial(reduce_kernel, sizes),
        out_shape=(block_shape, table_shape),
        in_specs=[SMEM, SMEM, SMEM, VMEM, VMEM],
        out_specs=(VMEM, VMEM),
        name="reduce",
    )(lower, upper, eigen_stream, span, blocks)

    by_core = ports.reshape(chips, 2, 4, height, LANES)
    chip, core = me // 2, me % 2
    kept = lax.dynamic_index_in_dim(by_core, core, 1, keepdims=False)
    given = lax.dynamic_index_in_dim(by_core, core ^ 1, 1, keepdims=False)
    taken = move(given, modes_by=1)
    chip_blocks = jnp.stack([kept, taken], axis=1)
    own, partner = [], []
    table_pair = move(table, pair=1)
    for d in range(chips):
        block = piece(chip_blocks, chip ^ d)
        own.append(move(block, modes_by=2 * d) if d else block)
        partner.append(move(block, modes_by=2 * d, pair=1))
    own_ports = jnp.concatenate(own, axis=0)
    pair_ports = jnp.concatenate(partner, axis=0)
    merged, pair_table = pl.pallas_call(
        functools.partial(merge_kernel, sizes),
        out_shape=(block_shape, table_shape),
        in_specs=[SMEM] + [VMEM] * 5,
        out_specs=(VMEM, VMEM),
        name="merge",
    )(eigen_stream, span, own_ports, pair_ports, table, table_pair)
    message = jnp.concatenate([merged.reshape(-1, LANES), pair_table], axis=0)
    others, tables = [], []
    for d in range(1, pairs):
        got = move(message, level=d)
        others.append(got[:-8].reshape(merged.shape))
        tables.append(got[-8:])
    sources = [piece(blocks, me)] + [move(piece(blocks, me ^ d), modes_by=d) for d in range(1, mode_count)]
    out = pl.pallas_call(
        functools.partial(final_kernel, sizes, pairs),
        out_shape=jax.ShapeDtypeStruct((rows, 2, mode_count, height, LANES), jnp.float32),
        in_specs=[SMEM] * 3 + [VMEM] * (3 + 2 * (pairs - 1) + mode_count),
        out_specs=VMEM,
        scratch_shapes=[pltpu.VMEM((rows, mode_count, height, LANES), jnp.float32)],
        name="solve",
    )(lower, upper, eigen_stream, span, pair_ports, table_pair, *others, *tables, *sources)
    out = out.reshape(rows, 2, mode_count * tiles, kx_count, LANES).transpose(0, 1, 3, 2, 4)
    return out.reshape(rows, 2, kx_count, -1)


def solution(mesh):
    in_specs = (P("gz", None, None, "modes"), P("gz"), P("gz"), P(), P())
    out_specs = P("gz", None, "modes", None)
    return jax.shard_map(
        per_device, mesh=mesh, in_specs=in_specs, out_specs=out_specs, check_vma=False
    )
```

time: 155 us -> 41.3 us (0.27)
  other arithmetic: 71 us -> 2.07 us
  between operations: 22.5 us -> 0.06 us
  local copies, waits for them, and re-layouts: 30.6 us -> 10.7 us
  starting transfers between devices: 23.1 us -> 13.3 us
  Pallas kernels: 0 us -> 7.24 us
    all_to_all x4 -> x0, starting transfers between devices: 21.8 us -> none  [the longest x1 7.67 us: per_device(): lax.all_to_all(right_items, 'gz', split_axis=3, concat_axis=0, tiled=True)]
    div x2 -> x0, other arithmetic: 17.7 us -> none  [the longest x1 17.7 us: thomas_forward(): factor = upper_val / pivots]
    sub x1 -> x0, other arithmetic: 17.6 us -> none  [thomas_forward(): pivots = lower_val + upper_val + spectral - lower_val * factor]
    unnamed x69 -> x19, local copies, waits for them, and re-layouts: 20.1 us -> 3.27 us
    unnamed x12 -> x0, other arithmetic: 16.4 us -> none
    add x3 -> x0, other arithmetic: 12.4 us -> none  [the longest x1 9.6 us: thomas_backward(): result = partial_value + factor * behind]
    ppermute x1 -> x11, starting transfers between devices: 1.29 us -> 13.3 us  [move(): return lax.ppermute(array, ('modes', 'gz'), links)]
    ppermute x1 -> x11, waiting for transfers between devices: 0.01 us -> 7.55 us  [move(): return lax.ppermute(array, ('modes', 'gz'), links)]
  transfers between devices with their start and end apart: 5 -> 11, of which waited for: 3 -> 4; matrix products, arithmetic and copies ran while one was open for 47% -> 12% of each run, Pallas kernels for 0% -> 0%
where the time goes in v1:
time: 41.3 us; the launch traced here: 40.9 us
  starting transfers between devices  13.3 us (32%)
  local copies, waits for them, and re-layouts  10.7 us (26%)
  waiting for transfers between devices  7.55 us (18%)
  Pallas kernels  7.24 us (18%)
  other arithmetic  2.07 us (5%)
    ppermute x11, starting transfers between devices, move(): return lax.ppermute(array, ('modes', 'gz'), links)  13.3 us
    ppermute x11, waiting for transfers between devices, move(): return lax.ppermute(array, ('modes', 'gz'), links)  7.55 us
    pallas_call x1, Pallas kernels, per_device(): pl.pallas_call(functools.partial(final_kernel, sizes, pairs), out_shape=j...  3.45 us
    unnamed x19, local copies, waits for them, and re-layouts  3.27 us
    reshape x2, local copies, waits for them, and re-layouts, per_device(): blocks = source_field.reshape(rows, 2, mode_count, kx_count, tiles, LANES)  2.27 us
    pallas_call x1, Pallas kernels, per_device(): pl.pallas_call(functools.partial(reduce_kernel, sizes), out_shape=(block_...  1.9 us
    pallas_call x1, Pallas kernels, per_device(): pl.pallas_call(functools.partial(merge_kernel, sizes), out_shape=(block_s...  1.89 us
    slice x3, local copies, waits for them, and re-layouts, per_device(): others.append(got[:-8].reshape(merged.shape))  1.88 us
  transfers between devices with their start and end apart: 11, of which 4 were waited for; matrix products, arithmetic and copies ran while one was open for 12% of the time, Pallas kernels for 0%

profile of v1, /device:TPU:0, one launch (start us, length us, event | category | flops | bytes accessed | tf_op | source)
XLA Modules:
  0.0 40.9 jit_solution(11194872460802752412)
XLA Ops:
  0.0 1.2 %reshape.31 = f32[16,2,4,2,4,128]{5,4,3,2,1,0:T(4,128)S(1)} reshape(f32[16,2,8,512]{3,2,1,0:T(8,128)} %param.5) | data formatting | bytes 1048576 | tf_op jit(solution)/shard_map/reshape | solution.py:235
  1.2 1.1 %copy.6 = f32[16,2,4,2,4,128]{5,3,4,1,0,2:T(2,128)} copy(f32[16,2,4,2,4,128]{5,4,3,2,1,0:T(4,128)S(1)} %reshape.31) | data formatting | bytes 1048576 | tf_op jit(solution)/shard_map/reshape | solution.py:235
  2.3 0.7 %copy-done.7 = f32[16]{0:T(128)S(1)} copy-done((f32[16]{0:T(128)S(1)}, f32[16]{0:T(128)}, u32[]{:S(2)}) %copy-start.7) | copy-done | bytes 88
  2.9 0.0 copy-done.8
  2.9 0.6 %compare_select_fusion = (f32[16]{0:T(128)}, f32[16]{0:T(128)}) fusion(f32[16]{0:T(128)S(1)} %copy-done.7, s32[]{:T(128)S(6)} %mul.3, f32[16]{0:T(128)S(1)} %copy-done.8), kind=kLoop, calls=%fused_computation.18 | loop fusion | flops 80 | bytes 260 | tf_op jit(solution)/shard_map/jit(_where)/select_n | solution.py:221
  3.5 1.9 %reduce.1 = (f32[4,4,8,128]{3,2,1,0:T(8,128)}, f32[8,128]{1,0:T(8,128)}) custom-call(f32[16]{0:T(128)} %get-tuple-element.22.lower_ref, f32[16]{0:T(128)} %get-tuple-element.21.upper_ref, f32[8]{0:T(128)} %stream_ref.5, f32[16,128]{1,0:T(8,128)} %bitcast.36, f32[4,16,2,8,128]{4,3,2,1,0:T(8,128)} %bitcast.31), custom_call_target="tpu_custom_call" | custom-call | tf_op jit(solution)/shard_map/reduce/pallas_call | solution.py:239
  5.5 0.8 %dynamic-slice_bitcast_fusion.4 = (f32[2,4,8,128]{3,2,1,0:T(8,128)S(1)}, f32[2,1,4,8,128]{4,3,2,1,0:T(8,128)S(1)}) fusion(f32[2,2,4,8,128]{4,3,2,1,0:T(8,128)} %bitcast.39, s32[]{:T(128)S(6)} %select_n.49, s32[]{:T(128)S(6)} %select_n.48), kind=kLoop, calls=%fused_computation.14 | loop fusion | bytes 131080 | tf_op jit(solution)/shard_map/jit(dynamic_index_in_dim)/squeeze | solution.py:250
  6.3 0.5 %collective-permute-start = (f32[2,4,8,128]{3,2,1,0:T(8,128)S(1)}, f32[2,4,8,128]{3,2,1,0:T(8,128)S(1)}, u32[]{:S(2)}, u32[]{:S(2)}) collective-permute-start(f32[2,4,8,128]{3,2,1,0:T(8,128)S(1)} %get-tuple-element.19), channel_id=1, source_target_pairs={{0,8},{1,9},{2,10},{3,11},{4,12},{5,13},{6,14},{7,15},{8,0},{9,1},... | collective-permute-start | bytes 98312 | tf_op jit(solution)/shard_map/ppermute | solution.py:230
  6.8 0.9 %collective-permute-done = f32[2,4,8,128]{3,2,1,0:T(8,128)S(1)} collective-permute-done((f32[2,4,8,128]{3,2,1,0:T(8,128)S(1)}, f32[2,4,8,128]{3,2,1,0:T(8,128)S(1)}, u32[]{:S(2)}, u32[]{:S(2)}) %collective-permute-start) | collective-permute-done | bytes 32800 | tf_op jit(solution)/shard_map/ppermute | solution.py:230
  7.7 2.9 %collective-permute-start.4 = (f32[2,4,8,128]{3,2,1,0:T(8,128)S(1)}, f32[2,4,8,128]{3,2,1,0:T(8,128)S(1)}, u32[]{:S(2)}, u32[]{:S(2)}) collective-permute-start(f32[2,4,8,128]{3,2,1,0:T(8,128)S(1)} %get-tuple-element.17), channel_id=1, source_target_pairs={{0,16},{1,17},{2,18},{3,19},{4,20},{5,21},{6,22},{7,23},{8,24},{9,... | collective-permute-start | bytes 98312 | tf_op jit(solution)/shard_map/ppermute | solution.py:230
  10.5 1.5 %collective-permute-start.3 = (f32[8,128]{1,0:T(8,128)}, f32[8,128]{1,0:T(8,128)S(1)}, u32[]{:S(2)}, u32[]{:S(2)}) collective-permute-start(f32[8,128]{1,0:T(8,128)} %get-tuple-element.10.own_table), channel_id=1, source_target_pairs={{0,1},{1,0},{2,3},{3,2},{4,5},{5,4},{6,7},{7,6},{8,9},{9,8},{10,11... | collective-permute-start | bytes 12296 | tf_op jit(solution)/shard_map/ppermute | solution.py:230
  12.0 0.0 collective-permute-start.2
  12.0 1.9 %collective-permute-start.1 = (f32[2,4,8,128]{3,2,1,0:T(8,128)S(1)}, f32[2,4,8,128]{3,2,1,0:T(8,128)S(1)}, u32[]{:S(2)}, u32[]{:S(2)}) collective-permute-start(f32[2,4,8,128]{3,2,1,0:T(8,128)S(1)} %get-tuple-element.18), channel_id=1, source_target_pairs={{0,1},{1,0},{2,3},{3,2},{4,5},{5,4},{6,7},{7,6},{8,9},{9,8},{10,11... | collective-permute-start | bytes 98312 | tf_op jit(solution)/shard_map/ppermute | solution.py:230
  14.0 0.0 collective-permute-done.4
  14.0 0.6 %pad_maximum_fusion.1.own_ref = f32[4,4,8,128]{3,2,1,0:T(8,128)} fusion(f32[2,4,8,128]{3,2,1,0:T(8,128)S(1)} %collective-permute-done.4, f32[2,4,8,128]{3,2,1,0:T(8,128)S(1)} %get-tuple-element.18), kind=kLoop, calls=%fused_computation.9 | loop fusion | flops 16384 | bytes 131072 | tf_op jit(solution)/shard_map/concatenate | solution.py:259
  14.6 1.6 %collective-permute-done.1 = f32[2,4,8,128]{3,2,1,0:T(8,128)S(1)} collective-permute-done((f32[2,4,8,128]{3,2,1,0:T(8,128)S(1)}, f32[2,4,8,128]{3,2,1,0:T(8,128)S(1)}, u32[]{:S(2)}, u32[]{:S(2)}) %collective-permute-start.1) | collective-permute-done | bytes 32800 | tf_op jit(solution)/shard_map/ppermute | solution.py:230
  16.2 0.6 %collective-permute-done.2 = f32[2,4,8,128]{3,2,1,0:T(8,128)S(1)} collective-permute-done((f32[2,4,8,128]{3,2,1,0:T(8,128)S(1)}, f32[2,4,8,128]{3,2,1,0:T(8,128)S(1)}, u32[]{:S(2)}, u32[]{:S(2)}) %collective-permute-start.2) | collective-permute-done | bytes 32800 | tf_op jit(solution)/shard_map/ppermute | solution.py:230
  16.8 0.0 collective-permute-done.3.pair_table
  16.8 0.6 %copy-done.1 = f32[4,4,8,128]{3,2,1,0:T(8,128)} copy-done((f32[4,4,8,128]{3,2,1,0:T(8,128)}, f32[4,4,8,128]{3,2,1,0:T(8,128)S(1)}, u32[]{:S(2)}) %copy-start.1) | copy-done | bytes 65560
  17.5 0.6 %copy-done.5 = f32[8,128]{1,0:T(8,128)} copy-done((f32[8,128]{1,0:T(8,128)}, f32[8,128]{1,0:T(8,128)S(1)}, u32[]{:S(2)}) %copy-start.5) | copy-done | bytes 4120
  18.0 1.9 %merge.1 = (f32[4,4,8,128]{3,2,1,0:T(8,128)}, f32[8,128]{1,0:T(8,128)}) custom-call(f32[8]{0:T(128)} %stream_ref.5, f32[16,128]{1,0:T(8,128)} %bitcast.37, f32[4,4,8,128]{3,2,1,0:T(8,128)} %pad_maximum_fusion.1.own_ref, f32[4,4,8,128]{3,2,1,0:T(8,128)} %copy-done.1, f32[8,128]{1,0:T(8,128)} %get-tuple-element.10.own_table, f32[8,128]{1,0:T(8,128)} %copy-done.5), custom_call_target="tpu_custom_call" | custom-call | tf_op jit(solution)/shard_map/merge/pallas_call | solution.py:261
  19.9 0.7 %copy-done.6 = f32[8,128]{1,0:T(8,128)S(1)} copy-done((f32[8,128]{1,0:T(8,128)S(1)}, f32[8,128]{1,0:T(8,128)}, u32[]{:S(2)}) %copy-start.6) | copy-done | bytes 4120
  20.6 0.8 %pad_maximum_fusion = f32[136,128]{1,0:T(8,128)S(1)} fusion(f32[8,128]{1,0:T(8,128)S(1)} %copy-done.6, f32[128,128]{1,0:T(8,128)} %bitcast.40), kind=kLoop, calls=%fused_computation.8 | loop fusion | flops 17408 | bytes 139264 | tf_op jit(solution)/shard_map/concatenate | solution.py:268
  21.4 3.6 %collective-permute-start.7 = (f32[136,128]{1,0:T(8,128)S(1)}, f32[136,128]{1,0:T(8,128)S(1)}, u32[]{:S(2)}, u32[]{:S(2)}) collective-permute-start(f32[136,128]{1,0:T(8,128)S(1)} %pad_maximum_fusion), channel_id=1, source_target_pairs={{0,6},{1,7},{2,0},{3,1},{4,2},{5,3},{6,4},{7,5},{8,14},{9,15},{10,... | collective-permute-start | bytes 208904 | tf_op jit(solution)/shard_map/ppermute | solution.py:230
  25.0 0.0 copy-done
  25.1 0.7 %dynamic-slice_bitcast_fusion = (f32[16,2,8,128]{3,2,1,0:T(8,128)S(1)}, f32[16,2,8,128]{3,2,1,0:T(8,128)S(1)}, f32[16,2,8,128]{3,2,1,0:T(8,128)S(1)}, f32[16,2,8,128]{3,2,1,0:T(8,128)}) fusion(f32[4,16,2,8,128]{4,3,2,1,0:T(8,128)S(1)} %bitcast.32, s32[]{:T(128)S(6)} %select_n.56, s32[]{:T(128)S(6)} %select_n.55, s32[]{:T(128)S(6)} %select_n.54, s32[]{:T(128)S(6)} %select_n.53), kind=kLoop, calls=%fused_computation | loop fusion | bytes 1048592 | tf_op jit(solution)/shard_map/jit(dynamic_index_in_dim)/squeeze | solution.py:233
  25.7 0.0 collective-permute-start.10
  25.7 1.1 %collective-permute-start.9 = (f32[16,2,8,128]{3,2,1,0:T(8,128)S(1)}, f32[16,2,8,128]{3,2,1,0:T(8,128)S(1)}, u32[]{:S(2)}, u32[]{:S(2)}) collective-permute-start(f32[16,2,8,128]{3,2,1,0:T(8,128)S(1)} %get-tuple-element.14), channel_id=1, source_target_pairs={{0,16},{1,17},{2,18},{3,19},{4,20},{5,21},{6,22},{7,23},{8,24},{9,... | collective-permute-start | bytes 393224 | tf_op jit(solution)/shard_map/ppermute | solution.py:230
  26.8 0.7 %collective-permute-start.8 = (f32[16,2,8,128]{3,2,1,0:T(8,128)S(1)}, f32[16,2,8,128]{3,2,1,0:T(8,128)S(1)}, u32[]{:S(2)}, u32[]{:S(2)}) collective-permute-start(f32[16,2,8,128]{3,2,1,0:T(8,128)S(1)} %get-tuple-element.15), channel_id=1, source_target_pairs={{0,8},{1,9},{2,10},{3,11},{4,12},{5,13},{6,14},{7,15},{8,0},{9,1},... | collective-permute-start | bytes 393224 | tf_op jit(solution)/shard_map/ppermute | solution.py:230
  27.6 0.0 collective-permute-start.6
  27.6 0.0 collective-permute-done.7
  27.6 1.0 %collective-permute-start.5 = (f32[136,128]{1,0:T(8,128)S(1)}, f32[136,128]{1,0:T(8,128)S(1)}, u32[]{:S(2)}, u32[]{:S(2)}) collective-permute-start(f32[136,128]{1,0:T(8,128)S(1)} %pad_maximum_fusion), channel_id=1, source_target_pairs={{0,2},{1,3},{2,4},{3,5},{4,6},{5,7},{6,0},{7,1},{8,10},{9,11},{10,... | collective-permute-start | bytes 208904 | tf_op jit(solution)/shard_map/ppermute | solution.py:230
  28.6 0.6 %slice.29.rest_5_ = f32[8,128]{1,0:T(8,128)} slice(f32[136,128]{1,0:T(8,128)S(1)} %collective-permute-done.7), slice={[128:136], [0:128]} | slice | bytes 8192 | tf_op jit(solution)/shard_map/slice | solution.py:273
  29.2 0.6 %slice.26 = f32[128,128]{1,0:T(8,128)} slice(f32[136,128]{1,0:T(8,128)S(1)} %collective-permute-done.7), slice={[0:128], [0:128]} | slice | bytes 131072 | tf_op jit(solution)/shard_map/slice | solution.py:272
  29.8 4.5 %collective-permute-done.6 = f32[136,128]{1,0:T(8,128)S(1)} collective-permute-done((f32[136,128]{1,0:T(8,128)S(1)}, f32[136,128]{1,0:T(8,128)S(1)}, u32[]{:S(2)}, u32[]{:S(2)}) %collective-permute-start.6) | collective-permute-done | bytes 69664 | tf_op jit(solution)/shard_map/ppermute | solution.py:230
  34.3 0.6 %slice.28.rest_4_ = f32[8,128]{1,0:T(8,128)} slice(f32[136,128]{1,0:T(8,128)S(1)} %collective-permute-done.6), slice={[128:136], [0:128]} | slice | bytes 8192 | tf_op jit(solution)/shard_map/slice | solution.py:273
  34.9 0.6 %slice.25 = f32[128,128]{1,0:T(8,128)} slice(f32[136,128]{1,0:T(8,128)S(1)} %collective-permute-done.6), slice={[0:128], [0:128]} | slice | bytes 131072 | tf_op jit(solution)/shard_map/slice | solution.py:272
  35.5 0.0 collective-permute-done.5
  35.5 0.6 %slice.27.rest_3_ = f32[8,128]{1,0:T(8,128)} slice(f32[136,128]{1,0:T(8,128)S(1)} %collective-permute-done.5), slice={[128:136], [0:128]} | slice | bytes 8192 | tf_op jit(solution)/shard_map/slice | solution.py:273
  36.1 0.6 %slice.24 = f32[128,128]{1,0:T(8,128)} slice(f32[136,128]{1,0:T(8,128)S(1)} %collective-permute-done.5), slice={[0:128], [0:128]} | slice | bytes 131072 | tf_op jit(solution)/shard_map/slice | solution.py:272
  36.7 0.0 collective-permute-done.10.rest_9_
  36.7 0.0 collective-permute-done.9.rest_8_
  36.7 0.0 copy-start.3
  36.7 0.0 collective-permute-done.8.rest_7_
  36.8 0.6 %copy-done.2 = f32[16,2,8,128]{3,2,1,0:T(8,128)} copy-done((f32[16,2,8,128]{3,2,1,0:T(8,128)}, f32[16,2,8,128]{3,2,1,0:T(8,128)S(1)}, u32[]{:S(2)}) %copy-start.2) | copy-done | bytes 131096
  37.4 0.1 copy-done.3
  37.4 0.0 copy-done.4
  37.5 3.5 %solve.1 = f32[16,2,4,8,128]{4,3,2,1,0:T(8,128)} custom-call(f32[16]{0:T(128)} %get-tuple-element.22.lower_ref, f32[16]{0:T(128)} %get-tuple-element.21.upper_ref, f32[8]{0:T(128)} %stream_ref.5, f32[16,128]{1,0:T(8,128)} %bitcast.38, f32[4,4,8,128]{3,2,1,0:T(8,128)} %copy-done.1, f32[8,128]{1,0:T(8,128)} %copy-done.5, f32[4,4,8,128]{3,2,1,0:T(8,128)} %bitcast.35, ...), custom_call_target="tpu_custom_call" | custom-call | tf_op jit(solution)/shard_map/solve/pallas_call | solution.py:275
  (11 shorter events, 0.0 us)
Async XLA Ops:
  2.3 0.7 %copy-start.7 = (f32[16]{0:T(128)S(1)}, f32[16]{0:T(128)}, u32[]{:S(2)}) copy-start(f32[16]{0:T(128)} %param.7) | copy-start | bytes 196
  2.3 0.7 %copy-start.8 = (f32[16]{0:T(128)S(1)}, f32[16]{0:T(128)}, u32[]{:S(2)}) copy-start(f32[16]{0:T(128)} %param.6) | copy-start | bytes 196
  5.5 19.6 %copy-start = (f32[16,2,4,2,4,128]{5,3,4,1,0,2:T(2,128)S(1)}, f32[16,2,4,2,4,128]{5,3,4,1,0,2:T(2,128)}, u32[]{:S(2)}) copy-start(f32[16,2,4,2,4,128]{5,3,4,1,0,2:T(2,128)} %copy.6) | copy-start | bytes 1572868
  6.3 1.4 %collective-permute-start = (f32[2,4,8,128]{3,2,1,0:T(8,128)S(1)}, f32[2,4,8,128]{3,2,1,0:T(8,128)S(1)}, u32[]{:S(2)}, u32[]{:S(2)}) collective-permute-start(f32[2,4,8,128]{3,2,1,0:T(8,128)S(1)} %get-tuple-element.19), channel_id=1, source_target_pairs={{0,8},{1,9},{2,10},{3,11},{4,12},{5,13},{6,14},{7,15},{8,0},{9,1},... | collective-permute-start | bytes 98312 | tf_op jit(solution)/shard_map/ppermute | solution.py:230
  7.7 6.3 %collective-permute-start.4 = (f32[2,4,8,128]{3,2,1,0:T(8,128)S(1)}, f32[2,4,8,128]{3,2,1,0:T(8,128)S(1)}, u32[]{:S(2)}, u32[]{:S(2)}) collective-permute-start(f32[2,4,8,128]{3,2,1,0:T(8,128)S(1)} %get-tuple-element.17), channel_id=1, source_target_pairs={{0,16},{1,17},{2,18},{3,19},{4,20},{5,21},{6,22},{7,23},{8,24},{9,... | collective-permute-start | bytes 98312 | tf_op jit(solution)/shard_map/ppermute | solution.py:230
  10.5 6.3 %collective-permute-start.3 = (f32[8,128]{1,0:T(8,128)}, f32[8,128]{1,0:T(8,128)S(1)}, u32[]{:S(2)}, u32[]{:S(2)}) collective-permute-start(f32[8,128]{1,0:T(8,128)} %get-tuple-element.10.own_table), channel_id=1, source_target_pairs={{0,1},{1,0},{2,3},{3,2},{4,5},{5,4},{6,7},{7,6},{8,9},{9,8},{10,11... | collective-permute-start | bytes 12296 | tf_op jit(solution)/shard_map/ppermute | solution.py:230
  12.0 4.8 %collective-permute-start.2 = (f32[2,4,8,128]{3,2,1,0:T(8,128)S(1)}, f32[2,4,8,128]{3,2,1,0:T(8,128)S(1)}, u32[]{:S(2)}, u32[]{:S(2)}) collective-permute-start(f32[2,4,8,128]{3,2,1,0:T(8,128)S(1)} %get-tuple-element.17), channel_id=1, source_target_pairs={{0,17},{1,16},{2,19},{3,18},{4,21},{5,20},{6,23},{7,22},{8,25},{9,... | collective-permute-start | bytes 98312 | tf_op jit(solution)/shard_map/ppermute | solution.py:230
  12.0 4.2 %collective-permute-start.1 = (f32[2,4,8,128]{3,2,1,0:T(8,128)S(1)}, f32[2,4,8,128]{3,2,1,0:T(8,128)S(1)}, u32[]{:S(2)}, u32[]{:S(2)}) collective-permute-start(f32[2,4,8,128]{3,2,1,0:T(8,128)S(1)} %get-tuple-element.18), channel_id=1, source_target_pairs={{0,1},{1,0},{2,3},{3,2},{4,5},{5,4},{6,7},{7,6},{8,9},{9,8},{10,11... | collective-permute-start | bytes 98312 | tf_op jit(solution)/shard_map/ppermute | solution.py:230
  16.8 0.6 %copy-start.1 = (f32[4,4,8,128]{3,2,1,0:T(8,128)}, f32[4,4,8,128]{3,2,1,0:T(8,128)S(1)}, u32[]{:S(2)}) copy-start(f32[4,4,8,128]{3,2,1,0:T(8,128)S(1)} %constant_dynamic-update-slice_fusion.pair_ref) | copy-start | bytes 196612
  17.4 0.6 %copy-start.5 = (f32[8,128]{1,0:T(8,128)}, f32[8,128]{1,0:T(8,128)S(1)}, u32[]{:S(2)}) copy-start(f32[8,128]{1,0:T(8,128)S(1)} %collective-permute-done.3.pair_table) | copy-start | bytes 12292
  19.9 0.7 %copy-start.6 = (f32[8,128]{1,0:T(8,128)S(1)}, f32[8,128]{1,0:T(8,128)}, u32[]{:S(2)}) copy-start(f32[8,128]{1,0:T(8,128)} %get-tuple-element.12) | copy-start | bytes 12292
  21.4 6.1 %collective-permute-start.7 = (f32[136,128]{1,0:T(8,128)S(1)}, f32[136,128]{1,0:T(8,128)S(1)}, u32[]{:S(2)}, u32[]{:S(2)}) collective-permute-start(f32[136,128]{1,0:T(8,128)S(1)} %pad_maximum_fusion), channel_id=1, source_target_pairs={{0,6},{1,7},{2,0},{3,1},{4,2},{5,3},{6,4},{7,5},{8,14},{9,15},{10,... | collective-permute-start | bytes 208904 | tf_op jit(solution)/shard_map/ppermute | solution.py:230
  25.7 11.0 %collective-permute-start.10 = (f32[16,2,8,128]{3,2,1,0:T(8,128)S(1)}, f32[16,2,8,128]{3,2,1,0:T(8,128)S(1)}, u32[]{:S(2)}, u32[]{:S(2)}) collective-permute-start(f32[16,2,8,128]{3,2,1,0:T(8,128)S(1)} %get-tuple-element.13), channel_id=1, source_target_pairs={{0,24},{1,25},{2,26},{3,27},{4,28},{5,29},{6,30},{7,31},{8,16},{9,... | collective-permute-start | bytes 393224 | tf_op jit(solution)/shard_map/ppermute | solution.py:230
  25.7 11.0 %collective-permute-start.9 = (f32[16,2,8,128]{3,2,1,0:T(8,128)S(1)}, f32[16,2,8,128]{3,2,1,0:T(8,128)S(1)}, u32[]{:S(2)}, u32[]{:S(2)}) collective-permute-start(f32[16,2,8,128]{3,2,1,0:T(8,128)S(1)} %get-tuple-element.14), channel_id=1, source_target_pairs={{0,16},{1,17},{2,18},{3,19},{4,20},{5,21},{6,22},{7,23},{8,24},{9,... | collective-permute-start | bytes 393224 | tf_op jit(solution)/shard_map/ppermute | solution.py:230
  26.8 9.9 %collective-permute-start.8 = (f32[16,2,8,128]{3,2,1,0:T(8,128)S(1)}, f32[16,2,8,128]{3,2,1,0:T(8,128)S(1)}, u32[]{:S(2)}, u32[]{:S(2)}) collective-permute-start(f32[16,2,8,128]{3,2,1,0:T(8,128)S(1)} %get-tuple-element.15), channel_id=1, source_target_pairs={{0,8},{1,9},{2,10},{3,11},{4,12},{5,13},{6,14},{7,15},{8,0},{9,1},... | collective-permute-start | bytes 393224 | tf_op jit(solution)/shard_map/ppermute | solution.py:230
  27.6 6.7 %collective-permute-start.6 = (f32[136,128]{1,0:T(8,128)S(1)}, f32[136,128]{1,0:T(8,128)S(1)}, u32[]{:S(2)}, u32[]{:S(2)}) collective-permute-start(f32[136,128]{1,0:T(8,128)S(1)} %pad_maximum_fusion), channel_id=1, source_target_pairs={{0,4},{1,5},{2,6},{3,7},{4,0},{5,1},{6,2},{7,3},{8,12},{9,13},{10,... | collective-permute-start | bytes 208904 | tf_op jit(solution)/shard_map/ppermute | solution.py:230
  27.6 7.9 %collective-permute-start.5 = (f32[136,128]{1,0:T(8,128)S(1)}, f32[136,128]{1,0:T(8,128)S(1)}, u32[]{:S(2)}, u32[]{:S(2)}) collective-permute-start(f32[136,128]{1,0:T(8,128)S(1)} %pad_maximum_fusion), channel_id=1, source_target_pairs={{0,2},{1,3},{2,4},{3,5},{4,6},{5,7},{6,0},{7,1},{8,10},{9,11},{10,... | collective-permute-start | bytes 208904 | tf_op jit(solution)/shard_map/ppermute | solution.py:230
  36.7 0.7 %copy-start.2 = (f32[16,2,8,128]{3,2,1,0:T(8,128)}, f32[16,2,8,128]{3,2,1,0:T(8,128)S(1)}, u32[]{:S(2)}) copy-start(f32[16,2,8,128]{3,2,1,0:T(8,128)S(1)} %collective-permute-done.10.rest_9_) | copy-start | bytes 393220
  36.7 0.7 %copy-start.3 = (f32[16,2,8,128]{3,2,1,0:T(8,128)}, f32[16,2,8,128]{3,2,1,0:T(8,128)S(1)}, u32[]{:S(2)}) copy-start(f32[16,2,8,128]{3,2,1,0:T(8,128)S(1)} %collective-permute-done.9.rest_8_) | copy-start | bytes 393220
  36.8 0.7 %copy-start.4 = (f32[16,2,8,128]{3,2,1,0:T(8,128)}, f32[16,2,8,128]{3,2,1,0:T(8,128)S(1)}, u32[]{:S(2)}) copy-start(f32[16,2,8,128]{3,2,1,0:T(8,128)S(1)} %collective-permute-done.8.rest_7_) | copy-start | bytes 393220
